TPU v7x, 512 devices: a whole 4x4x16 slice. The times are simulated.
512 devices in a mesh: dp: 32 (over z, core), seq: 16 (over y, x).
Axes of the slice: x: 4, y: 4, z: 16, core: 2. Of those that a mesh axis runs over, the one named last changes fastest.
Arguments:
- q_pre: bfloat16 [32, 2048, 16, 128], P('dp', 'seq'), may hold values from -6 to 6
- k_pre: bfloat16 [32, 2048, 8, 128], P('dp', 'seq'), may hold values from -6 to 6
- values: bfloat16 [32, 2048, 8, 128], P('dp', 'seq'), may hold values from -6 to 6
- grad_out: bfloat16 [32, 2048, 16, 128], P('dp', 'seq'), may hold values from -6 to 6
- segment_ids: int32 [32, 2048], P('dp', 'seq'), may hold values from 0 to 7, never falling along the last dimension, each value on 1 to 1024 neighbouring positions
- q_gain: float32 [128], replicated, may hold values from 0.1 to 1.9
- k_gain: float32 [128], replicated, may hold values from 0.1 to 1.9
Outputs:
- grad_q: bfloat16 [32, 2048, 16, 128], P('dp', 'seq')
- grad_k: bfloat16 [32, 2048, 8, 128], P('dp', 'seq')
- grad_v: bfloat16 [32, 2048, 8, 128], P('dp', 'seq')
- grad_q_gain: float32 [128], replicated
- grad_k_gain: float32 [128], replicated
Inputs may be any that keep to these rules, and one draw needn't show every extreme that they name: `segment_ids`: along a span the ids never fall, and each id from 0 to 7 names one run of consecutive tokens.
All inputs are finite; a program needn't handle non-finite values.
Results may differ from a plain program's by a relative error of at most 0.017.
Values may be sent and summed in bfloat16 or wider, within the bound.
A program may use at most 64 MiB of HBM per device.

v0:
```python
import jax
import jax.numpy as jnp
from jax import lax
from jax.sharding import PartitionSpec as P

PRESCALE = 168
DOCS = 8
norm_epsilon = 1e-06
rope_base = 1000000.0
rope_factor = 8.0


def document_positions(segments, docs):
    labels = jnp.arange(docs, dtype=jnp.int32)
    member = (segments[:, None] == labels[None, :]).astype(jnp.int32)
    counts = jnp.sum(member, axis=0)
    starts = jnp.cumsum(counts) - counts
    first = jnp.sum(member * starts[None, :], axis=1)
    return (jnp.arange(segments.shape[0], dtype=jnp.int32) - first, first)


def embed(rows, gain, positions):
    width = rows.shape[-1]
    half = width // 2
    scale = lax.rsqrt(jnp.mean(rows * rows, axis=-1, keepdims=True) + norm_epsilon)
    normed = rows * scale * gain
    freqs = rope_base ** (-(jnp.arange(half, dtype=jnp.float32) * 2.0 / width))
    angles = (positions.astype(jnp.float32) / rope_factor)[:, None] * freqs[None, :]
    cosine = jnp.cos(angles)[:, None, :]
    sine = jnp.sin(angles)[:, None, :]
    first_half = normed[..., :half]
    second_half = normed[..., half:]
    return jnp.concatenate(
        [first_half * cosine - second_half * sine, second_half * cosine + first_half * sine],
        axis=-1,
    )


def attend_blocks(queries, keys, vals, upstream, segments):
    total = queries.shape[0]
    group = queries.shape[1]
    width = queries.shape[2]
    block = min(512, total)
    count = total // block
    rows = block * group
    score_scale = float(PRESCALE) ** (-0.5)
    contract_last = (((1,), (1,)), ((), ()))
    contract_first = (((0,), (0,)), ((), ()))

    def query_block(query_index, carry):
        query_grads, key_grads, value_grads = carry
        start = query_index * block
        query_rows = lax.dynamic_slice_in_dim(queries, start, block, 0).reshape(rows, width)
        upstream_rows = lax.dynamic_slice_in_dim(upstream, start, block, 0).reshape(rows, width)
        query_segs = jnp.repeat(lax.dynamic_slice_in_dim(segments, start, block, 0), group)
        query_places = jnp.repeat(start + jnp.arange(block, dtype=jnp.int32), group)
        lower = 0

        def key_scores(key_index):
            key_start = key_index * block
            key_rows = lax.dynamic_slice_in_dim(keys, key_start, block, 0)
            value_rows = lax.dynamic_slice_in_dim(vals, key_start, block, 0)
            key_segs = lax.dynamic_slice_in_dim(segments, key_start, block, 0)
            key_places = key_start + jnp.arange(block, dtype=jnp.int32)
            scores = score_scale * lax.dot_general(
                query_rows, key_rows, contract_last, preferred_element_type=jnp.float32
            )
            visible = (query_segs[:, None] == key_segs[None, :]) & (
                query_places[:, None] >= key_places[None, :]
            )
            return (scores, visible, key_rows, value_rows, key_start)

        def forward_step(key_index, state):
            totals, numer = state
            scores, visible, key_rows, value_rows, key_start = key_scores(key_index)
            raw = jnp.where(visible, jnp.exp(scores), 0.0)
            numer = numer + jnp.dot(
                raw.astype(jnp.bfloat16), value_rows, preferred_element_type=jnp.float32
            )
            return (totals + jnp.sum(raw, axis=1), numer)

        totals, numer = lax.fori_loop(
            lower,
            query_index + 1,
            forward_step,
            (jnp.zeros((rows,), jnp.float32), jnp.zeros((rows, width), jnp.float32)),
        )
        outputs = numer / totals[:, None]
        delta = jnp.sum(upstream_rows.astype(jnp.float32) * outputs, axis=1)
        logsum = jnp.log(totals)

        def backward_step(key_index, state):
            query_part, key_acc, value_acc = state
            scores, visible, key_rows, value_rows, key_start = key_scores(key_index)
            probs = jnp.where(visible, jnp.exp(scores - logsum[:, None]), 0.0).astype(jnp.bfloat16)
            prob_grads = lax.dot_general(
                upstream_rows, value_rows, contract_last, preferred_element_type=jnp.float32
            )
            score_grads = (
                probs.astype(jnp.float32) * (prob_grads - delta[:, None]) * score_scale
            ).astype(jnp.bfloat16)
            query_part = query_part + jnp.dot(
                score_grads, key_rows, preferred_element_type=jnp.float32
            )
            key_part = lax.dot_general(
                score_grads, query_rows, contract_first, preferred_element_type=jnp.float32
            )
            value_part = lax.dot_general(
                probs, upstream_rows, contract_first, preferred_element_type=jnp.float32
            )
            key_acc = lax.dynamic_update_slice_in_dim(
                key_acc,
                lax.dynamic_slice_in_dim(key_acc, key_start, block, 0) + key_part,
                key_start,
                0,
            )
            value_acc = lax.dynamic_update_slice_in_dim(
                value_acc,
                lax.dynamic_slice_in_dim(value_acc, key_start, block, 0) + value_part,
                key_start,
                0,
            )
            return (query_part, key_acc, value_acc)

        query_part, key_grads, value_grads = lax.fori_loop(
            lower,
            query_index + 1,
            backward_step,
            (jnp.zeros((rows, width), jnp.float32), key_grads, value_grads),
        )
        query_grads = lax.dynamic_update_slice_in_dim(query_grads, query_part, start * group, 0)
        return (query_grads, key_grads, value_grads)

    initial = (
        jnp.zeros((total * group, width), jnp.float32),
        jnp.zeros((total, width), jnp.float32),
        jnp.zeros((total, width), jnp.float32),
    )
    query_grads, key_grads, value_grads = lax.fori_loop(0, count, query_block, initial)
    return (query_grads.reshape(total, group, width), key_grads, value_grads)


def body(q_pre, k_pre, values, grad_out, segment_ids, q_gain, k_gain):
    segments = lax.all_gather(segment_ids, "seq", axis=1, tiled=True)[0]
    positions, first = document_positions(segments, DOCS)
    local = q_pre.shape[1]
    heads = q_pre.shape[2]
    kv_heads = k_pre.shape[2]
    width = q_pre.shape[3]
    group = heads // kv_heads

    def embed_rows(rows, gain):
        return embed(rows, gain, positions)

    key_copies = jnp.repeat(k_pre[0], group, axis=1)
    value_copies = jnp.repeat(values[0], group, axis=1)
    query_here, upstream_here, key_here, value_here = (
        lax.all_to_all(q_pre[0], "seq", split_axis=1, concat_axis=0, tiled=True),
        lax.all_to_all(grad_out[0], "seq", split_axis=1, concat_axis=0, tiled=True),
        lax.all_to_all(key_copies, "seq", split_axis=1, concat_axis=0, tiled=True),
        lax.all_to_all(value_copies, "seq", split_axis=1, concat_axis=0, tiled=True),
    )
    query_rot, query_back = jax.vjp(embed_rows, query_here.astype(jnp.float32), q_gain)
    key_rot, key_back = jax.vjp(embed_rows, key_here.astype(jnp.float32), k_gain)
    query_hat = query_rot.astype(jnp.bfloat16)
    key_hat = key_rot.astype(jnp.bfloat16)
    query_list, key_list, value_list = ([], [], [])
    query_part, key_part, value_part = attend_blocks(
        query_hat, key_hat[:, 0], value_here[:, 0], upstream_here, segments
    )
    query_list.append(query_part)
    key_list.append(key_part)
    value_list.append(value_part)
    query_input, query_gain_part = query_back(query_list[0])
    key_input, key_gain_part = key_back(jnp.stack(key_list, axis=1))
    value_input = jnp.stack(value_list, axis=1)
    query_return, key_return, value_return = (
        lax.all_to_all(
            query_input.astype(jnp.bfloat16), "seq", split_axis=0, concat_axis=1, tiled=True
        ).astype(query_input.dtype),
        lax.all_to_all(
            key_input.astype(jnp.bfloat16), "seq", split_axis=0, concat_axis=1, tiled=True
        ).astype(key_input.dtype),
        lax.all_to_all(
            value_input.astype(jnp.bfloat16), "seq", split_axis=0, concat_axis=1, tiled=True
        ).astype(value_input.dtype),
    )
    grad_q = query_return.astype(jnp.bfloat16)
    grad_k = jnp.sum(key_return.reshape(local, kv_heads, group, width), axis=2).astype(jnp.bfloat16)
    grad_v = jnp.sum(value_return.reshape(local, kv_heads, group, width), axis=2).astype(
        jnp.bfloat16
    )
    gain_totals = lax.psum((query_gain_part, key_gain_part), ("dp", "seq"))
    return (grad_q[None], grad_k[None], grad_v[None], gain_totals[0], gain_totals[1])


def solution(mesh):
    return jax.shard_map(
        body,
        mesh=mesh,
        in_specs=(
            P("dp", "seq", None, None),
            P("dp", "seq", None, None),
            P("dp", "seq", None, None),
            P("dp", "seq", None, None),
            P("dp", "seq"),
            P(),
            P(),
        ),
        out_specs=(
            P("dp", "seq", None, None),
            P("dp", "seq", None, None),
            P("dp", "seq", None, None),
            P(),
            P(),
        ),
        check_vma=False,
    )
```

profile of v0, /device:TPU:1, one launch (start us, length us, event | category | flops | bytes accessed | tf_op | source)
XLA Modules:
  0.0 308.5 jit_solution(509402824562934716)
XLA Ops:
  0.6 2.0 copy.172
  2.6 7.7 %all-to-all-start = ((bf16[128,16,128]{2,0,1:T(8,128)(2,1)}), bf16[128,16,128]{2,0,1:T(8,128)(2,1)S(1)}, u32[]{:S(2)}, u32[]{:S(2)}) async-start(bf16[128,16,128]{2,0,1:T(8,128)(2,1)} %bitcast.130), calls=%async_computation | async-start | bytes 1048576 | tf_op jit(solution)/shard_map/all_to_all | solution.py:158
  10.4 17.6 %all_gather.3 = s32[1,2048]{1,0:T(1,128)S(1)} all-gather(s32[1,128]{1,0:T(1,128)S(1)} %copy-done.13), channel_id=1, replica_groups=mesh['dp'=32,'seq'=16] {'seq'}, dimensions={1}, use_global_device_ids=true | all-gather | bytes 8704 | tf_op jit(solution)/shard_map/all_gather | solution.py:144
  31.3 4.0 %all-to-all-start.1 = ((bf16[128,16,128]{0,2,1:T(8,128)(2,1)}), bf16[128,16,128]{0,2,1:T(8,128)(2,1)S(1)}, u32[]{:S(2)}, u32[]{:S(2)}) async-start(bf16[128,16,128]{0,2,1:T(8,128)(2,1)} %bitcast.12), calls=%async_computation.1 | async-start | bytes 1048576 | tf_op jit(solution)/shard_map/all_to_all | solution.py:160
  37.4 6.9 %all-to-all-done.1 = bf16[128,16,128]{0,2,1:T(8,128)(2,1)S(1)} async-done(((bf16[128,16,128]{0,2,1:T(8,128)(2,1)}), bf16[128,16,128]{0,2,1:T(8,128)(2,1)S(1)}, u32[]{:S(2)}, u32[]{:S(2)}) %all-to-all-start.1) | async-done | bytes 524320 | tf_op jit(solution)/shard_map/all_to_all | solution.py:160
  45.3 3.6 %all-to-all-start.2 = ((bf16[128,16,128]{2,0,1:T(8,128)(2,1)}), bf16[128,16,128]{2,0,1:T(8,128)(2,1)S(1)}, u32[]{:S(2)}, u32[]{:S(2)}) async-start(bf16[128,16,128]{2,0,1:T(8,128)(2,1)} %bitcast.20), calls=%async_computation.2 | async-start | bytes 1048576 | tf_op jit(solution)/shard_map/all_to_all | solution.py:161
  50.8 7.0 %all-to-all-done.2 = bf16[128,16,128]{2,0,1:T(8,128)(2,1)S(1)} async-done(((bf16[128,16,128]{2,0,1:T(8,128)(2,1)}), bf16[128,16,128]{2,0,1:T(8,128)(2,1)S(1)}, u32[]{:S(2)}, u32[]{:S(2)}) %all-to-all-start.2) | async-done | bytes 524320 | tf_op jit(solution)/shard_map/all_to_all | solution.py:161
  57.8 4.2 %all-to-all-start.3 = ((bf16[128,16,128]{2,0,1:T(8,128)(2,1)}), bf16[128,16,128]{2,0,1:T(8,128)(2,1)}, u32[]{:S(2)}, u32[]{:S(2)}) async-start(bf16[128,16,128]{2,0,1:T(8,128)(2,1)} %bitcast.129), calls=%async_computation.3 | async-start | bytes 1048576 | tf_op jit(solution)/shard_map/all_to_all | solution.py:159
  62.1 3.1 fusion.63
  66.2 4.8 %all-to-all-done.3 = bf16[128,16,128]{2,0,1:T(8,128)(2,1)} async-done(((bf16[128,16,128]{2,0,1:T(8,128)(2,1)}), bf16[128,16,128]{2,0,1:T(8,128)(2,1)}, u32[]{:S(2)}, u32[]{:S(2)}) %all-to-all-start.3) | async-done | bytes 524320 | tf_op jit(solution)/shard_map/all_to_all | solution.py:159
  72.3 69.1 %while.79 = (s32[]{:T(128)}, f32[2048,128]{0,1:T(8,128)}, f32[2048,128]{1,0:T(8,128)S(1)}, f32[2048,128]{1,0:T(8,128)S(1)}, bf16[2048,1,128]{0,2,1:T(8,128)(2,1)...) while((s32[]{:T(128)}, f32[2048,128]{0,1:T(8,128)}, ...), condition=%wide.region_12.13_spmd, body=%wide.region_5.12_spmd.sunk | while | flops 475268608 | bytes 14478353 | solution.py:139
  73.2 1.9 while.80
  73.3 1.4 fusion.101
  76.3 3.7 %while.81 = (s32[]{:T(128)}, f32[512,128]{1,0:T(8,128)S(1)}, f32[2048,128]{1,0:T(8,128)S(1)}, f32[2048,128]{1,0:T(8,128)S(1)}, s32[]{:T(128)}, /*index=5*/s32[51...) while((s32[]{:T(128)}, f32[512,128]{1,0:T(8,128)S(1)}, ...), condition=%wide.region_11.11_spmd.clone, body=%wide.region_10.10_spmd.clone.sunk | while | flops 338887680 | bytes 5656819 | solution.py:125
  76.4 1.4 fusion.112
  82.1 3.7 %while.80 = (s32[]{:T(128)}, f32[512]{0:T(512)S(1)}, f32[512,128]{1,0:T(8,128)S(1)}, s32[]{:T(128)}, s32[512]{0:T(512)S(1)}, /*index=5*/s32[2048]{0:T(1024)S(1)}...) while((s32[]{:T(128)}, f32[512]{0:T(512)S(1)}, ...), condition=%wide.region_8.8_spmd.clone, body=%wide.region_6.7_spmd.clone.sunk | while | flops 136119296 | bytes 1990855 | solution.py:82
  82.2 1.4 fusion.101
  84.1 1.4 fusion.101
  87.0 7.4 %while.81 = (s32[]{:T(128)}, f32[512,128]{1,0:T(8,128)S(1)}, f32[2048,128]{1,0:T(8,128)S(1)}, f32[2048,128]{1,0:T(8,128)S(1)}, s32[]{:T(128)}, /*index=5*/s32[51...) while((s32[]{:T(128)}, f32[512,128]{1,0:T(8,128)S(1)}, ...), condition=%wide.region_11.11_spmd.clone, body=%wide.region_10.10_spmd.clone.sunk | while | flops 338887680 | bytes 5656819 | solution.py:125
  87.1 1.4 fusion.112
  89.5 1.3 convolution_add_fusion.7
  90.9 1.4 fusion.112
  96.6 5.6 %while.80 = (s32[]{:T(128)}, f32[512]{0:T(512)S(1)}, f32[512,128]{1,0:T(8,128)S(1)}, s32[]{:T(128)}, s32[512]{0:T(512)S(1)}, /*index=5*/s32[2048]{0:T(1024)S(1)}...) while((s32[]{:T(128)}, f32[512]{0:T(512)S(1)}, ...), condition=%wide.region_8.8_spmd.clone, body=%wide.region_6.7_spmd.clone.sunk | while | flops 136119296 | bytes 1990855 | solution.py:82
  96.7 1.4 fusion.101
  98.6 1.4 fusion.101
  100.4 1.4 fusion.101
  103.4 11.1 %while.81 = (s32[]{:T(128)}, f32[512,128]{1,0:T(8,128)S(1)}, f32[2048,128]{1,0:T(8,128)S(1)}, f32[2048,128]{1,0:T(8,128)S(1)}, s32[]{:T(128)}, /*index=5*/s32[51...) while((s32[]{:T(128)}, f32[512,128]{1,0:T(8,128)S(1)}, ...), condition=%wide.region_11.11_spmd.clone, body=%wide.region_10.10_spmd.clone.sunk | while | flops 338887680 | bytes 5656819 | solution.py:125
  103.5 1.4 fusion.112
  107.2 1.4 fusion.112
  110.9 1.4 fusion.112
  116.6 7.5 %while.80 = (s32[]{:T(128)}, f32[512]{0:T(512)S(1)}, f32[512,128]{1,0:T(8,128)S(1)}, s32[]{:T(128)}, s32[512]{0:T(512)S(1)}, /*index=5*/s32[2048]{0:T(1024)S(1)}...) while((s32[]{:T(128)}, f32[512]{0:T(512)S(1)}, ...), condition=%wide.region_8.8_spmd.clone, body=%wide.region_6.7_spmd.clone.sunk | while | flops 136119296 | bytes 1990855 | solution.py:82
  116.7 1.4 fusion.101
  118.6 1.4 fusion.101
  120.5 1.4 fusion.101
  122.3 1.4 fusion.101
  125.3 14.8 %while.81 = (s32[]{:T(128)}, f32[512,128]{1,0:T(8,128)S(1)}, f32[2048,128]{1,0:T(8,128)S(1)}, f32[2048,128]{1,0:T(8,128)S(1)}, s32[]{:T(128)}, /*index=5*/s32[51...) while((s32[]{:T(128)}, f32[512,128]{1,0:T(8,128)S(1)}, ...), condition=%wide.region_11.11_spmd.clone, body=%wide.region_10.10_spmd.clone.sunk | while | flops 338887680 | bytes 5656819 | solution.py:125
  125.4 1.4 fusion.112
  129.1 1.4 fusion.112
  132.8 1.4 fusion.112
  136.5 1.4 fusion.112
  141.4 1.3 copy.139
  142.7 4.1 %fusion.60 = (f32[2048,1,64]{0,2,1:T(8,128)S(1)}, f32[2048,1,64]{0,2,1:T(8,128)S(1)}, f32[2048,1,64]{0,2,1:T(8,128)S(1)}, f32[2048,1,64]{0,2,1:T(8,128)S(1)}) fusion(f32[2048,1,128]{0,2,1:T(8,128)} %bitcast.158, f32[64]{0:T(128)S(1)} %negate_power_fusion, f32[2048]{0:T(1024)S(1)} %convert_multiply_fusion.1, f32[2048,1,128]{0,2,1:T(8,128)} %bitcast.157), kind=kLoop, calls=%fused_computation.89 | loop fusion | flops 1966080 | bytes 4202752 | tf_op jit(solution)/shard_map/transpose(jvp())/add_any | solution.py:34
  151.6 3.6 %all-to-all-start.4 = ((bf16[16,2,8192]{2,1,0:T(2,128)(2,1)}), bf16[16,2,8192]{2,1,0:T(2,128)(2,1)S(1)}, u32[]{:S(2)}, u32[]{:S(2)}) async-start(bf16[16,2,8192]{2,1,0:T(2,128)(2,1)} %reshape.576), calls=%async_computation.4 | async-start | bytes 1048576 | tf_op jit(solution)/shard_map/all_to_all | solution.py:178
  157.4 6.8 %all-to-all-done.4 = bf16[16,2,8192]{2,1,0:T(2,128)(2,1)S(1)} async-done(((bf16[16,2,8192]{2,1,0:T(2,128)(2,1)}), bf16[16,2,8192]{2,1,0:T(2,128)(2,1)S(1)}, u32[]{:S(2)}, u32[]{:S(2)}) %all-to-all-start.4) | async-done | bytes 524320 | tf_op jit(solution)/shard_map/all_to_all | solution.py:178
  164.1 3.6 %all-to-all-start.5 = ((bf16[16,2,8192]{2,1,0:T(2,128)(2,1)}), bf16[16,2,8192]{2,1,0:T(2,128)(2,1)S(1)}, u32[]{:S(2)}, u32[]{:S(2)}) async-start(bf16[16,2,8192]{2,1,0:T(2,128)(2,1)} %reshape.578), calls=%async_computation.5 | async-start | bytes 1048576 | tf_op jit(solution)/shard_map/all_to_all | solution.py:181
  169.7 9.0 %all-to-all-done.5 = bf16[16,2,8192]{2,1,0:T(2,128)(2,1)S(1)} async-done(((bf16[16,2,8192]{2,1,0:T(2,128)(2,1)}), bf16[16,2,8192]{2,1,0:T(2,128)(2,1)S(1)}, u32[]{:S(2)}, u32[]{:S(2)}) %all-to-all-start.5) | async-done | bytes 524320 | tf_op jit(solution)/shard_map/all_to_all | solution.py:181
  178.7 3.6 %all-to-all-start.6 = ((bf16[16,2,8192]{2,1,0:T(2,128)(2,1)}), bf16[16,2,8192]{2,1,0:T(2,128)(2,1)S(1)}, u32[]{:S(2)}, u32[]{:S(2)}) async-start(bf16[16,2,8192]{2,1,0:T(2,128)(2,1)} %reshape.580), calls=%async_computation.6 | async-start | bytes 1048576 | tf_op jit(solution)/shard_map/all_to_all | solution.py:184
  182.3 121.2 %all-reduce.4 = (f32[128]{0:T(128)}, f32[128]{0:T(128)}) all-reduce(f32[128]{0:T(128)S(1)} %get-tuple-element.430, f32[128]{0:T(128)S(1)} %get-tuple-element.428), channel_id=1, replica_groups=mesh['dp'=32,'seq'=16] {'dp','seq'}, use_global_device_ids=true, to_apply=%region_18.19 | all-reduce | flops 256 | bytes 2048 | tf_op jit(solution)/shard_map/psum | solution.py:193
  (232 shorter events, 63.7 us)
Async XLA Ops:
  2.6 7.7 %copy-start.13 = (s32[1,128]{1,0:T(1,128)S(1)}, s32[1,128]{1,0:T(1,128)}, u32[]{:S(2)}) copy-start(s32[1,128]{1,0:T(1,128)} %param.17) | copy-start | bytes 1540
  2.6 25.7 %copy-start.9 = (bf16[1,128,8,128]{3,2,1,0:T(8,128)(2,1)S(1)}, bf16[1,128,8,128]{3,2,1,0:T(8,128)(2,1)}, u32[]{:S(2)}) copy-start(bf16[1,128,8,128]{3,2,1,0:T(8,128)(2,1)} %param.14) | copy-start | bytes 786436
  2.6 27.8 %all-to-all-start = ((bf16[128,16,128]{2,0,1:T(8,128)(2,1)}), bf16[128,16,128]{2,0,1:T(8,128)(2,1)S(1)}, u32[]{:S(2)}, u32[]{:S(2)}) async-start(bf16[128,16,128]{2,0,1:T(8,128)(2,1)} %bitcast.130), calls=%async_computation | async-start | bytes 1048576 | tf_op jit(solution)/shard_map/all_to_all | solution.py:158
  10.3 18.2 %copy-start.10 = (bf16[1,128,8,128]{3,2,1,0:T(8,128)(2,1)S(1)}, bf16[1,128,8,128]{3,2,1,0:T(8,128)(2,1)}, u32[]{:S(2)}) copy-start(bf16[1,128,8,128]{3,2,1,0:T(8,128)(2,1)} %param.15) | copy-start | bytes 786436
  28.3 1.0 copy-start.8
  31.3 13.0 %all-to-all-start.1 = ((bf16[128,16,128]{0,2,1:T(8,128)(2,1)}), bf16[128,16,128]{0,2,1:T(8,128)(2,1)S(1)}, u32[]{:S(2)}, u32[]{:S(2)}) async-start(bf16[128,16,128]{0,2,1:T(8,128)(2,1)} %bitcast.12), calls=%async_computation.1 | async-start | bytes 1048576 | tf_op jit(solution)/shard_map/all_to_all | solution.py:160
  35.8 0.7 copy-start.12
  36.5 1.0 copy-start
  44.3 4.7 %copy-start.2 = (bf16[128,16,128]{0,2,1:T(8,128)(2,1)}, bf16[128,16,128]{0,2,1:T(8,128)(2,1)S(1)}, u32[]{:S(2)}) copy-start(bf16[128,16,128]{0,2,1:T(8,128)(2,1)S(1)} %all-to-all-done.1) | copy-start | bytes 1572868
  45.3 12.5 %all-to-all-start.2 = ((bf16[128,16,128]{2,0,1:T(8,128)(2,1)}), bf16[128,16,128]{2,0,1:T(8,128)(2,1)S(1)}, u32[]{:S(2)}, u32[]{:S(2)}) async-start(bf16[128,16,128]{2,0,1:T(8,128)(2,1)} %bitcast.20), calls=%async_computation.2 | async-start | bytes 1048576 | tf_op jit(solution)/shard_map/all_to_all | solution.py:161
  49.0 0.7 copy-start.11
  50.8 11.2 %copy-start.4 = (f32[2048,1,128]{0,2,1:T(8,128)S(1)}, f32[2048,1,128]{0,2,1:T(8,128)}, u32[]{:S(2)}) copy-start(f32[2048,1,128]{0,2,1:T(8,128)} %fusion.33) | copy-start | bytes 3145732
  57.8 13.2 %all-to-all-start.3 = ((bf16[128,16,128]{2,0,1:T(8,128)(2,1)}), bf16[128,16,128]{2,0,1:T(8,128)(2,1)}, u32[]{:S(2)}, u32[]{:S(2)}) async-start(bf16[128,16,128]{2,0,1:T(8,128)(2,1)} %bitcast.129), calls=%async_computation.3 | async-start | bytes 1048576 | tf_op jit(solution)/shard_map/all_to_all | solution.py:159
  65.2 1.0 copy-start.7
  72.4 0.8 copy-start.5
  80.1 1.1 copy-start.6
  81.3 0.8 copy-start.5
  94.6 1.1 copy-start.6
  95.7 0.8 copy-start.5
  114.6 1.1 copy-start.6
  115.8 0.8 copy-start.5
  140.3 1.1 copy-start.6
  142.7 4.1 %copy-start.3 = (bf16[128,16,128]{0,2,1:T(8,128)(2,1)S(1)}, bf16[128,16,128]{0,2,1:T(8,128)(2,1)}, u32[]{:S(2)}) copy-start(bf16[128,16,128]{0,2,1:T(8,128)(2,1)} %copy-done.2) | copy-start | bytes 1572868
  146.8 1.2 copy-start.1
  151.6 12.5 %all-to-all-start.4 = ((bf16[16,2,8192]{2,1,0:T(2,128)(2,1)}), bf16[16,2,8192]{2,1,0:T(2,128)(2,1)S(1)}, u32[]{:S(2)}, u32[]{:S(2)}) async-start(bf16[16,2,8192]{2,1,0:T(2,128)(2,1)} %reshape.576), calls=%async_computation.4 | async-start | bytes 1048576 | tf_op jit(solution)/shard_map/all_to_all | solution.py:178
  164.1 14.6 %all-to-all-start.5 = ((bf16[16,2,8192]{2,1,0:T(2,128)(2,1)}), bf16[16,2,8192]{2,1,0:T(2,128)(2,1)S(1)}, u32[]{:S(2)}, u32[]{:S(2)}) async-start(bf16[16,2,8192]{2,1,0:T(2,128)(2,1)} %reshape.578), calls=%async_computation.5 | async-start | bytes 1048576 | tf_op jit(solution)/shard_map/all_to_all | solution.py:181
  178.7 128.1 %all-to-all-start.6 = ((bf16[16,2,8192]{2,1,0:T(2,128)(2,1)}), bf16[16,2,8192]{2,1,0:T(2,128)(2,1)S(1)}, u32[]{:S(2)}, u32[]{:S(2)}) async-start(bf16[16,2,8192]{2,1,0:T(2,128)(2,1)} %reshape.580), calls=%async_computation.6 | async-start | bytes 1048576 | tf_op jit(solution)/shard_map/all_to_all | solution.py:184
where the time goes:
time: 310 us; the launch traced here: 308 us
  blocking collectives  139 us (45%)
  matrix products  53.1 us (17%)
  waiting for transfers between devices  34.4 us (11%)
  local copies, waits for them, and re-layouts  30.6 us (10%)
  starting transfers between devices  30.2 us (10%)
  other arithmetic  19 us (6%)
    psum x1, blocking collectives, body(): gain_totals = lax.psum((query_gain_part, key_gain_part), ('dp', 'seq'))  121 us
    dot_general x20, matrix products, key_scores(): lax.dot_general(query_rows, key_rows, contract_last, preferred_element_ty...  27.3 us
    all_gather x1, blocking collectives, body(): segments = lax.all_gather(segment_ids, 'seq', axis=1, tiled=True)[0]  17.6 us
    unnamed x40, local copies, waits for them, and re-layouts  14.1 us
    dot_general x10, matrix products, backward_step(): jnp.dot(score_grads, key_rows, preferred_element_type=jnp.float32)  12.8 us
    all_to_all x1, waiting for transfers between devices, body(): lax.all_to_all(key_input.astype(jnp.bfloat16), 'seq', split_axis=0, conca...  8.96 us
    all_to_all x1, starting transfers between devices, body(): lax.all_to_all(q_pre[0], 'seq', split_axis=1, concat_axis=0, tiled=True)  7.72 us
    all_to_all x1, waiting for transfers between devices, body(): lax.all_to_all(value_copies, 'seq', split_axis=1, concat_axis=0, tiled=True)  6.98 us
  transfers between devices with their start and end apart: 7, of which 5 were waited for; matrix products, arithmetic and copies ran while one was open for 5% of the time, Pallas kernels for 0%

commit v1 on v0

--- a/solution.py
+++ b/solution.py
@@ -190,7 +190,7 @@
     grad_v = jnp.sum(value_return.reshape(local, kv_heads, group, width), axis=2).astype(
         jnp.bfloat16
     )
-    gain_totals = lax.psum((query_gain_part, key_gain_part), ("dp", "seq"))
+    gain_totals = lax.psum(lax.psum((query_gain_part, key_gain_part), "dp"), "seq")
     return (grad_q[None], grad_k[None], grad_v[None], gain_totals[0], gain_totals[1])
 
 

time: 310 us -> 291 us (0.939); the launches traced: 308 us -> 286 us
  blocking collectives: 139 us -> 117 us
    psum x1 -> x2, blocking collectives: 121 us -> 99 us  [the longest x1 65.3 us: body(): lax.psum((query_gain_part, key_gain_part), 'dp')]
where the time goes in v1:
time: 291 us; the launch traced here: 286 us
  blocking collectives  117 us (40%)
  matrix products  53.1 us (18%)
  waiting for transfers between devices  34.4 us (12%)
  local copies, waits for them, and re-layouts  30.6 us (11%)
  starting transfers between devices  30.2 us (10%)
  other arithmetic  19 us (7%)
    psum x1, blocking collectives, body(): lax.psum((query_gain_part, key_gain_part), 'dp')  65.3 us
    psum x1, blocking collectives, body(): lax.psum(lax.psum((query_gain_part, key_gain_part), 'dp'), 'seq')  33.7 us
    dot_general x20, matrix products, key_scores(): lax.dot_general(query_rows, key_rows, contract_last, preferred_element_ty...  27.3 us
    all_gather x1, blocking collectives, body(): segments = lax.all_gather(segment_ids, 'seq', axis=1, tiled=True)[0]  17.6 us
    unnamed x40, local copies, waits for them, and re-layouts  14.1 us
    dot_general x10, matrix products, backward_step(): jnp.dot(score_grads, key_rows, preferred_element_type=jnp.float32)  12.8 us
    all_to_all x1, waiting for transfers between devices, body(): lax.all_to_all(key_input.astype(jnp.bfloat16), 'seq', split_axis=0, conca...  8.96 us
    all_to_all x1, starting transfers between devices, body(): lax.all_to_all(q_pre[0], 'seq', split_axis=1, concat_axis=0, tiled=True)  7.72 us
  transfers between devices with their start and end apart: 7, of which 5 were waited for; matrix products, arithmetic and copies ran while one was open for 5% of the time, Pallas kernels for 0%

profile of v1, /device:TPU:1, one launch (start us, length us, event | category | flops | bytes accessed | tf_op | source)
XLA Modules:
  0.0 286.3 jit_solution(9093472283838568308)
XLA Ops:
  0.6 2.0 copy.172
  2.6 7.7 %all-to-all-start = ((bf16[128,16,128]{2,0,1:T(8,128)(2,1)}), bf16[128,16,128]{2,0,1:T(8,128)(2,1)S(1)}, u32[]{:S(2)}, u32[]{:S(2)}) async-start(bf16[128,16,128]{2,0,1:T(8,128)(2,1)} %bitcast.130), calls=%async_computation | async-start | bytes 1048576 | tf_op jit(solution)/shard_map/all_to_all | solution.py:158
  10.4 17.6 %all_gather.3 = s32[1,2048]{1,0:T(1,128)S(1)} all-gather(s32[1,128]{1,0:T(1,128)S(1)} %copy-done.13), channel_id=1, replica_groups=mesh['dp'=32,'seq'=16] {'seq'}, dimensions={1}, use_global_device_ids=true | all-gather | bytes 8704 | tf_op jit(solution)/shard_map/all_gather | solution.py:144
  31.3 4.0 %all-to-all-start.1 = ((bf16[128,16,128]{0,2,1:T(8,128)(2,1)}), bf16[128,16,128]{0,2,1:T(8,128)(2,1)S(1)}, u32[]{:S(2)}, u32[]{:S(2)}) async-start(bf16[128,16,128]{0,2,1:T(8,128)(2,1)} %bitcast.12), calls=%async_computation.1 | async-start | bytes 1048576 | tf_op jit(solution)/shard_map/all_to_all | solution.py:160
  37.4 6.9 %all-to-all-done.1 = bf16[128,16,128]{0,2,1:T(8,128)(2,1)S(1)} async-done(((bf16[128,16,128]{0,2,1:T(8,128)(2,1)}), bf16[128,16,128]{0,2,1:T(8,128)(2,1)S(1)}, u32[]{:S(2)}, u32[]{:S(2)}) %all-to-all-start.1) | async-done | bytes 524320 | tf_op jit(solution)/shard_map/all_to_all | solution.py:160
  45.3 3.6 %all-to-all-start.2 = ((bf16[128,16,128]{2,0,1:T(8,128)(2,1)}), bf16[128,16,128]{2,0,1:T(8,128)(2,1)S(1)}, u32[]{:S(2)}, u32[]{:S(2)}) async-start(bf16[128,16,128]{2,0,1:T(8,128)(2,1)} %bitcast.20), calls=%async_computation.2 | async-start | bytes 1048576 | tf_op jit(solution)/shard_map/all_to_all | solution.py:161
  50.8 7.0 %all-to-all-done.2 = bf16[128,16,128]{2,0,1:T(8,128)(2,1)S(1)} async-done(((bf16[128,16,128]{2,0,1:T(8,128)(2,1)}), bf16[128,16,128]{2,0,1:T(8,128)(2,1)S(1)}, u32[]{:S(2)}, u32[]{:S(2)}) %all-to-all-start.2) | async-done | bytes 524320 | tf_op jit(solution)/shard_map/all_to_all | solution.py:161
  57.8 4.2 %all-to-all-start.3 = ((bf16[128,16,128]{2,0,1:T(8,128)(2,1)}), bf16[128,16,128]{2,0,1:T(8,128)(2,1)}, u32[]{:S(2)}, u32[]{:S(2)}) async-start(bf16[128,16,128]{2,0,1:T(8,128)(2,1)} %bitcast.129), calls=%async_computation.3 | async-start | bytes 1048576 | tf_op jit(solution)/shard_map/all_to_all | solution.py:159
  62.1 3.1 %fusion.63 = (bf16[2048,64]{0,1:T(8,128)(2,1)S(1)}, bf16[2048,64]{0,1:T(8,128)(2,1)S(1)}, bf16[2048,1,64]{0,2,1:T(8,128)(2,1)S(1)}, bf16[2048,1,64]{0,2,1:T(8,128)(2,1)}) fusion(f32[2048,1,128]{0,2,1:T(8,128)S(1)} %copy-done.4, f32[64]{0:T(128)S(1)} %negate_power_fusion, f32[2048]{0:T(1024)S(1)} %convert_multiply_fusion.1, ...), kind=kLoop, calls=%fused_computation.97 | loop fusion | flops 2228224 | bytes 3154176 | tf_op jit(solution)/shard_map/jvp()/concatenate | solution.py:33
  66.2 4.8 %all-to-all-done.3 = bf16[128,16,128]{2,0,1:T(8,128)(2,1)} async-done(((bf16[128,16,128]{2,0,1:T(8,128)(2,1)}), bf16[128,16,128]{2,0,1:T(8,128)(2,1)}, u32[]{:S(2)}, u32[]{:S(2)}) %all-to-all-start.3) | async-done | bytes 524320 | tf_op jit(solution)/shard_map/all_to_all | solution.py:159
  72.3 69.1 %while.79 = (s32[]{:T(128)}, f32[2048,128]{0,1:T(8,128)}, f32[2048,128]{1,0:T(8,128)S(1)}, f32[2048,128]{1,0:T(8,128)S(1)}, bf16[2048,1,128]{0,2,1:T(8,128)(2,1)...) while((s32[]{:T(128)}, f32[2048,128]{0,1:T(8,128)}, ...), condition=%wide.region_12.13_spmd, body=%wide.region_5.12_spmd.sunk | while | flops 475268608 | bytes 14478353 | solution.py:139
  73.2 1.9 while.80
  73.3 1.4 fusion.101
  76.3 3.7 %while.81 = (s32[]{:T(128)}, f32[512,128]{1,0:T(8,128)S(1)}, f32[2048,128]{1,0:T(8,128)S(1)}, f32[2048,128]{1,0:T(8,128)S(1)}, s32[]{:T(128)}, /*index=5*/s32[51...) while((s32[]{:T(128)}, f32[512,128]{1,0:T(8,128)S(1)}, ...), condition=%wide.region_11.11_spmd.clone, body=%wide.region_10.10_spmd.clone.sunk | while | flops 338887680 | bytes 5656819 | solution.py:125
  76.4 1.4 fusion.112
  82.1 3.7 %while.80 = (s32[]{:T(128)}, f32[512]{0:T(512)S(1)}, f32[512,128]{1,0:T(8,128)S(1)}, s32[]{:T(128)}, s32[512]{0:T(512)S(1)}, /*index=5*/s32[2048]{0:T(1024)S(1)}...) while((s32[]{:T(128)}, f32[512]{0:T(512)S(1)}, ...), condition=%wide.region_8.8_spmd.clone, body=%wide.region_6.7_spmd.clone.sunk | while | flops 136119296 | bytes 1990855 | solution.py:82
  82.2 1.4 fusion.101
  84.1 1.4 fusion.101
  87.0 7.4 %while.81 = (s32[]{:T(128)}, f32[512,128]{1,0:T(8,128)S(1)}, f32[2048,128]{1,0:T(8,128)S(1)}, f32[2048,128]{1,0:T(8,128)S(1)}, s32[]{:T(128)}, /*index=5*/s32[51...) while((s32[]{:T(128)}, f32[512,128]{1,0:T(8,128)S(1)}, ...), condition=%wide.region_11.11_spmd.clone, body=%wide.region_10.10_spmd.clone.sunk | while | flops 338887680 | bytes 5656819 | solution.py:125
  87.1 1.4 fusion.112
  90.9 1.4 fusion.112
  96.6 5.6 %while.80 = (s32[]{:T(128)}, f32[512]{0:T(512)S(1)}, f32[512,128]{1,0:T(8,128)S(1)}, s32[]{:T(128)}, s32[512]{0:T(512)S(1)}, /*index=5*/s32[2048]{0:T(1024)S(1)}...) while((s32[]{:T(128)}, f32[512]{0:T(512)S(1)}, ...), condition=%wide.region_8.8_spmd.clone, body=%wide.region_6.7_spmd.clone.sunk | while | flops 136119296 | bytes 1990855 | solution.py:82
  96.7 1.4 fusion.101
  98.6 1.4 fusion.101
  100.4 1.4 fusion.101
  103.4 11.1 %while.81 = (s32[]{:T(128)}, f32[512,128]{1,0:T(8,128)S(1)}, f32[2048,128]{1,0:T(8,128)S(1)}, f32[2048,128]{1,0:T(8,128)S(1)}, s32[]{:T(128)}, /*index=5*/s32[51...) while((s32[]{:T(128)}, f32[512,128]{1,0:T(8,128)S(1)}, ...), condition=%wide.region_11.11_spmd.clone, body=%wide.region_10.10_spmd.clone.sunk | while | flops 338887680 | bytes 5656819 | solution.py:125
  103.5 1.4 fusion.112
  107.2 1.4 fusion.112
  110.9 1.4 fusion.112
  116.6 7.5 %while.80 = (s32[]{:T(128)}, f32[512]{0:T(512)S(1)}, f32[512,128]{1,0:T(8,128)S(1)}, s32[]{:T(128)}, s32[512]{0:T(512)S(1)}, /*index=5*/s32[2048]{0:T(1024)S(1)}...) while((s32[]{:T(128)}, f32[512]{0:T(512)S(1)}, ...), condition=%wide.region_8.8_spmd.clone, body=%wide.region_6.7_spmd.clone.sunk | while | flops 136119296 | bytes 1990855 | solution.py:82
  116.7 1.4 fusion.101
  118.6 1.4 fusion.101
  120.5 1.4 fusion.101
  122.3 1.4 fusion.101
  125.3 14.8 %while.81 = (s32[]{:T(128)}, f32[512,128]{1,0:T(8,128)S(1)}, f32[2048,128]{1,0:T(8,128)S(1)}, f32[2048,128]{1,0:T(8,128)S(1)}, s32[]{:T(128)}, /*index=5*/s32[51...) while((s32[]{:T(128)}, f32[512,128]{1,0:T(8,128)S(1)}, ...), condition=%wide.region_11.11_spmd.clone, body=%wide.region_10.10_spmd.clone.sunk | while | flops 338887680 | bytes 5656819 | solution.py:125
  125.4 1.4 fusion.112
  129.1 1.4 fusion.112
  132.8 1.4 fusion.112
  136.5 1.4 fusion.112
  141.4 1.3 copy.139
  142.7 4.1 %fusion.60 = (f32[2048,1,64]{0,2,1:T(8,128)S(1)}, f32[2048,1,64]{0,2,1:T(8,128)S(1)}, f32[2048,1,64]{0,2,1:T(8,128)S(1)}, f32[2048,1,64]{0,2,1:T(8,128)S(1)}) fusion(f32[2048,1,128]{0,2,1:T(8,128)} %bitcast.158, f32[64]{0:T(128)S(1)} %negate_power_fusion, f32[2048]{0:T(1024)S(1)} %convert_multiply_fusion.1, f32[2048,1,128]{0,2,1:T(8,128)} %bitcast.157), kind=kLoop, calls=%fused_computation.89 | loop fusion | flops 1966080 | bytes 4202752 | tf_op jit(solution)/shard_map/transpose(jvp())/add_any | solution.py:34
  151.6 3.6 %all-to-all-start.4 = ((bf16[16,2,8192]{2,1,0:T(2,128)(2,1)}), bf16[16,2,8192]{2,1,0:T(2,128)(2,1)S(1)}, u32[]{:S(2)}, u32[]{:S(2)}) async-start(bf16[16,2,8192]{2,1,0:T(2,128)(2,1)} %reshape.576), calls=%async_computation.4 | async-start | bytes 1048576 | tf_op jit(solution)/shard_map/all_to_all | solution.py:178
  157.4 6.8 %all-to-all-done.4 = bf16[16,2,8192]{2,1,0:T(2,128)(2,1)S(1)} async-done(((bf16[16,2,8192]{2,1,0:T(2,128)(2,1)}), bf16[16,2,8192]{2,1,0:T(2,128)(2,1)S(1)}, u32[]{:S(2)}, u32[]{:S(2)}) %all-to-all-start.4) | async-done | bytes 524320 | tf_op jit(solution)/shard_map/all_to_all | solution.py:178
  164.1 3.6 %all-to-all-start.5 = ((bf16[16,2,8192]{2,1,0:T(2,128)(2,1)}), bf16[16,2,8192]{2,1,0:T(2,128)(2,1)S(1)}, u32[]{:S(2)}, u32[]{:S(2)}) async-start(bf16[16,2,8192]{2,1,0:T(2,128)(2,1)} %reshape.578), calls=%async_computation.5 | async-start | bytes 1048576 | tf_op jit(solution)/shard_map/all_to_all | solution.py:181
  169.7 9.0 %all-to-all-done.5 = bf16[16,2,8192]{2,1,0:T(2,128)(2,1)S(1)} async-done(((bf16[16,2,8192]{2,1,0:T(2,128)(2,1)}), bf16[16,2,8192]{2,1,0:T(2,128)(2,1)S(1)}, u32[]{:S(2)}, u32[]{:S(2)}) %all-to-all-start.5) | async-done | bytes 524320 | tf_op jit(solution)/shard_map/all_to_all | solution.py:181
  178.7 3.6 %all-to-all-start.6 = ((bf16[16,2,8192]{2,1,0:T(2,128)(2,1)}), bf16[16,2,8192]{2,1,0:T(2,128)(2,1)S(1)}, u32[]{:S(2)}, u32[]{:S(2)}) async-start(bf16[16,2,8192]{2,1,0:T(2,128)(2,1)} %reshape.580), calls=%async_computation.6 | async-start | bytes 1048576 | tf_op jit(solution)/shard_map/all_to_all | solution.py:184
  182.3 65.3 %all-reduce.4 = (f32[128]{0:T(128)S(1)}, f32[128]{0:T(128)S(1)}) all-reduce(f32[128]{0:T(128)S(1)} %get-tuple-element.430, f32[128]{0:T(128)S(1)} %get-tuple-element.428), channel_id=1, replica_groups=mesh['dp'=32,'seq'=16] {'dp'}, use_global_device_ids=true, to_apply=%region_18.19 | all-reduce | flops 256 | bytes 2048 | tf_op jit(solution)/shard_map/psum | solution.py:193
  247.6 33.7 %all-reduce.5 = (f32[128]{0:T(128)}, f32[128]{0:T(128)}) all-reduce(f32[128]{0:T(128)S(1)} %get-tuple-element.498, f32[128]{0:T(128)S(1)} %get-tuple-element.499), channel_id=1, replica_groups=mesh['dp'=32,'seq'=16] {'seq'}, use_global_device_ids=true, to_apply=%region_19.20 | all-reduce | flops 256 | bytes 2048 | tf_op jit(solution)/shard_map/psum | solution.py:193
  (233 shorter events, 65.0 us)
Async XLA Ops:
  2.6 7.7 %copy-start.13 = (s32[1,128]{1,0:T(1,128)S(1)}, s32[1,128]{1,0:T(1,128)}, u32[]{:S(2)}) copy-start(s32[1,128]{1,0:T(1,128)} %param.17) | copy-start | bytes 1540
  2.6 25.7 %copy-start.9 = (bf16[1,128,8,128]{3,2,1,0:T(8,128)(2,1)S(1)}, bf16[1,128,8,128]{3,2,1,0:T(8,128)(2,1)}, u32[]{:S(2)}) copy-start(bf16[1,128,8,128]{3,2,1,0:T(8,128)(2,1)} %param.14) | copy-start | bytes 786436
  2.6 27.8 %all-to-all-start = ((bf16[128,16,128]{2,0,1:T(8,128)(2,1)}), bf16[128,16,128]{2,0,1:T(8,128)(2,1)S(1)}, u32[]{:S(2)}, u32[]{:S(2)}) async-start(bf16[128,16,128]{2,0,1:T(8,128)(2,1)} %bitcast.130), calls=%async_computation | async-start | bytes 1048576 | tf_op jit(solution)/shard_map/all_to_all | solution.py:158
  10.3 18.2 %copy-start.10 = (bf16[1,128,8,128]{3,2,1,0:T(8,128)(2,1)S(1)}, bf16[1,128,8,128]{3,2,1,0:T(8,128)(2,1)}, u32[]{:S(2)}) copy-start(bf16[1,128,8,128]{3,2,1,0:T(8,128)(2,1)} %param.15) | copy-start | bytes 786436
  28.3 1.0 copy-start.8
  31.3 13.0 %all-to-all-start.1 = ((bf16[128,16,128]{0,2,1:T(8,128)(2,1)}), bf16[128,16,128]{0,2,1:T(8,128)(2,1)S(1)}, u32[]{:S(2)}, u32[]{:S(2)}) async-start(bf16[128,16,128]{0,2,1:T(8,128)(2,1)} %bitcast.12), calls=%async_computation.1 | async-start | bytes 1048576 | tf_op jit(solution)/shard_map/all_to_all | solution.py:160
  35.8 0.7 copy-start.12
  36.5 1.0 copy-start
  44.3 4.7 %copy-start.2 = (bf16[128,16,128]{0,2,1:T(8,128)(2,1)}, bf16[128,16,128]{0,2,1:T(8,128)(2,1)S(1)}, u32[]{:S(2)}) copy-start(bf16[128,16,128]{0,2,1:T(8,128)(2,1)S(1)} %all-to-all-done.1) | copy-start | bytes 1572868
  45.3 12.5 %all-to-all-start.2 = ((bf16[128,16,128]{2,0,1:T(8,128)(2,1)}), bf16[128,16,128]{2,0,1:T(8,128)(2,1)S(1)}, u32[]{:S(2)}, u32[]{:S(2)}) async-start(bf16[128,16,128]{2,0,1:T(8,128)(2,1)} %bitcast.20), calls=%async_computation.2 | async-start | bytes 1048576 | tf_op jit(solution)/shard_map/all_to_all | solution.py:161
  49.0 0.7 copy-start.11
  50.8 11.2 %copy-start.4 = (f32[2048,1,128]{0,2,1:T(8,128)S(1)}, f32[2048,1,128]{0,2,1:T(8,128)}, u32[]{:S(2)}) copy-start(f32[2048,1,128]{0,2,1:T(8,128)} %fusion.33) | copy-start | bytes 3145732
  57.8 13.2 %all-to-all-start.3 = ((bf16[128,16,128]{2,0,1:T(8,128)(2,1)}), bf16[128,16,128]{2,0,1:T(8,128)(2,1)}, u32[]{:S(2)}, u32[]{:S(2)}) async-start(bf16[128,16,128]{2,0,1:T(8,128)(2,1)} %bitcast.129), calls=%async_computation.3 | async-start | bytes 1048576 | tf_op jit(solution)/shard_map/all_to_all | solution.py:159
  65.2 1.0 copy-start.7
  72.4 0.8 copy-start.5
  80.1 1.1 copy-start.6
  81.3 0.8 copy-start.5
  94.6 1.1 copy-start.6
  95.7 0.8 copy-start.5
  114.6 1.1 copy-start.6
  115.8 0.8 copy-start.5
  140.3 1.1 copy-start.6
  142.7 4.1 %copy-start.3 = (bf16[128,16,128]{0,2,1:T(8,128)(2,1)S(1)}, bf16[128,16,128]{0,2,1:T(8,128)(2,1)}, u32[]{:S(2)}) copy-start(bf16[128,16,128]{0,2,1:T(8,128)(2,1)} %copy-done.2) | copy-start | bytes 1572868
  146.8 1.2 copy-start.1
  151.6 12.5 %all-to-all-start.4 = ((bf16[16,2,8192]{2,1,0:T(2,128)(2,1)}), bf16[16,2,8192]{2,1,0:T(2,128)(2,1)S(1)}, u32[]{:S(2)}, u32[]{:S(2)}) async-start(bf16[16,2,8192]{2,1,0:T(2,128)(2,1)} %reshape.576), calls=%async_computation.4 | async-start | bytes 1048576 | tf_op jit(solution)/shard_map/all_to_all | solution.py:178
  164.1 14.6 %all-to-all-start.5 = ((bf16[16,2,8192]{2,1,0:T(2,128)(2,1)}), bf16[16,2,8192]{2,1,0:T(2,128)(2,1)S(1)}, u32[]{:S(2)}, u32[]{:S(2)}) async-start(bf16[16,2,8192]{2,1,0:T(2,128)(2,1)} %reshape.578), calls=%async_computation.5 | async-start | bytes 1048576 | tf_op jit(solution)/shard_map/all_to_all | solution.py:181
  178.7 106.0 %all-to-all-start.6 = ((bf16[16,2,8192]{2,1,0:T(2,128)(2,1)}), bf16[16,2,8192]{2,1,0:T(2,128)(2,1)S(1)}, u32[]{:S(2)}, u32[]{:S(2)}) async-start(bf16[16,2,8192]{2,1,0:T(2,128)(2,1)} %reshape.580), calls=%async_computation.6 | async-start | bytes 1048576 | tf_op jit(solution)/shard_map/all_to_all | solution.py:184
